TPU v7x, 32 devices: a whole 2x2x4 slice. The times are simulated.
32 devices in a mesh: dp: 16 (over z, x, core), rep: 2 (over y).
Axes of the slice: x: 2, y: 2, z: 4, core: 2. Of those that a mesh axis runs over, the one named last changes fastest.
Arguments:
- learn_residual: bfloat16 [20480, 1024], P(('dp', 'rep')), may hold values from -6 to 6
- learn_hidden: bfloat16 [20480, 4096], P(('dp', 'rep')), may hold values from -6 to 6
- fresh_residual: bfloat16 [20480, 1024], P(('dp', 'rep')), may hold values from -6 to 6
- fresh_hidden: bfloat16 [20480, 4096], P(('dp', 'rep')), may hold values from -6 to 6
- down_weight: bfloat16 [4096, 1024], P('dp'), may hold values from -0.09375 to 0.09375
- head_weight: bfloat16 [1024, 19], replicated, may hold values from -0.1875 to 0.1875
- norm_gain: bfloat16 [1024], replicated, may hold values from 0.099609375 to 1.8984375
- actions: int32 [256, 80], P(('dp', 'rep')), may hold values from 0 to 17
- behaviour_logits: float32 [20480, 18], P(('dp', 'rep')), may hold values from -6 to 6
- rewards: float32 [256, 80], P(('dp', 'rep')), may hold values from -6 to 6
- episode_done: int32 [256, 80], P(('dp', 'rep')), may hold values 0 or 1
- lengths: int32 [256], P(('dp', 'rep')), may hold values from 40 to 80, as said below
- bootstrap: float32 [256], P(('dp', 'rep')), may hold values from -6 to 6
Outputs:
- fresh_policy: float32 [20480, 19], P(('dp', 'rep'))
- learn_targets: float32 [256, 80], P(('dp', 'rep'))
- hidden_grad: bfloat16 [20480, 4096], P(('dp', 'rep'))
- down_grad: float32 [4096, 1024], P('dp')
- head_grad: float32 [1024, 19], replicated
- gain_grad: float32 [1024], replicated
Inputs may be any that keep to these rules, and one draw needn't show every extreme that they name: `lengths`: on at least one device all 8 trajectories of that device have the full 80 steps.
All inputs are finite; a program needn't handle non-finite values. No bound on the sum of `episode_done` on one device may be relied on, other than what follows from the above.
Results may differ from a plain program's by a relative error of at most 0.0049.
Values may be sent and summed in bfloat16 or wider, within the bound.
A program may use at most 128 MiB of HBM per device.

v0:
```python
import jax
import jax.numpy as jnp
from jax import lax
from jax.sharding import PartitionSpec as P

ACTIONS = 18
STEPS = 80
TRAJ_DEV = 8
DISCOUNT = 0.99
BASELINE_COST = 0.5
ENTROPY_COST = 0.05
EPSILON = 1e-05


def normalize(features, gain_vector):
    inverse_rms = lax.rsqrt(jnp.mean(features * features, axis=1, keepdims=True) + EPSILON)
    return features * inverse_rms * gain_vector[None, :]


def head_outputs(features, head_matrix, gain_vector):
    return jnp.dot(normalize(features, gain_vector), head_matrix, precision=lax.Precision.HIGHEST)


def log_policy(logits):
    return logits - jnp.log(jnp.sum(jnp.exp(logits), axis=-1, keepdims=True))


def compose_steps(earlier, later):
    return (earlier[0] * later[0], later[1] + later[0] * earlier[1])


def trace_returns(errors, traces):
    _, corrections = lax.associative_scan(compose_steps, (traces, errors), reverse=True, axis=1)
    return corrections


def learner_loss(
    features,
    head_matrix,
    gain_vector,
    actions,
    behaviour_logits,
    rewards,
    episode_done,
    lengths,
    bootstrap,
):
    trajectories = actions.shape[0]
    outputs = head_outputs(features, head_matrix, gain_vector)
    logprob = log_policy(outputs[:, :ACTIONS])
    values = outputs[:, ACTIONS].reshape(trajectories, STEPS)
    one_hot = (
        actions.reshape(-1)[:, None] == jnp.arange(ACTIONS, dtype=jnp.int32)[None, :]
    ).astype(jnp.float32)
    taken = jnp.sum(logprob * one_hot, axis=1).reshape(trajectories, STEPS)
    behaved = jnp.sum(log_policy(behaviour_logits) * one_hot, axis=1).reshape(trajectories, STEPS)
    entropy = -jnp.sum(jnp.exp(logprob) * logprob, axis=1).reshape(trajectories, STEPS)
    clipped_ratio = jnp.minimum(1.0, jnp.exp(lax.stop_gradient(taken) - behaved))
    positions = jnp.arange(STEPS, dtype=jnp.int32)[None, :]
    inside = positions < lengths[:, None]
    final_step = positions == lengths[:, None] - 1
    discounts = DISCOUNT * (1.0 - episode_done.astype(jnp.float32))
    baseline = lax.stop_gradient(values)
    empty_column = jnp.zeros((trajectories, 1), jnp.float32)
    next_value = jnp.concatenate([baseline[:, 1:], empty_column], axis=1)
    next_value = jnp.where(final_step, bootstrap[:, None], next_value)
    errors = jnp.where(inside, clipped_ratio * (rewards + discounts * next_value - baseline), 0.0)
    traces = jnp.where(inside, discounts * clipped_ratio, 0.0)
    targets = baseline + trace_returns(errors, traces)
    next_target = jnp.concatenate([targets[:, 1:], empty_column], axis=1)
    next_target = jnp.where(final_step, bootstrap[:, None], next_target)
    advantage = clipped_ratio * (rewards + discounts * next_target - baseline)
    per_step = (
        -advantage * taken + 0.5 * BASELINE_COST * (targets - values) ** 2 - ENTROPY_COST * entropy
    )
    total_loss = jnp.sum(jnp.where(inside, per_step, 0.0)) / (TRAJ_DEV * STEPS)
    return (total_loss, targets)


def local(
    learn_residual,
    learn_hidden,
    fresh_residual,
    fresh_hidden,
    down_weight,
    head_weight,
    norm_gain,
    actions,
    behaviour_logits,
    rewards,
    episode_done,
    lengths,
    bootstrap,
):
    head_matrix = head_weight.astype(jnp.float32)
    gain_vector = norm_gain.astype(jnp.float32)
    full_down = lax.all_gather(down_weight, "dp", axis=0, tiled=True)
    learn_stream = learn_residual.astype(jnp.float32) + jnp.dot(
        learn_hidden, full_down, preferred_element_type=jnp.float32
    )
    fresh_stream = fresh_residual.astype(jnp.float32) + jnp.dot(
        fresh_hidden, full_down, preferred_element_type=jnp.float32
    )
    fresh_policy = head_outputs(fresh_stream, head_matrix, gain_vector)

    def loss_of(features, head_values, gain_values):
        return learner_loss(
            features,
            head_values,
            gain_values,
            actions,
            behaviour_logits,
            rewards,
            episode_done,
            lengths,
            bootstrap,
        )

    total_loss, pullback, targets = jax.vjp(
        loss_of, learn_stream, head_matrix, gain_vector, has_aux=True
    )
    stream_grad, head_local, gain_local = pullback(jnp.ones_like(total_loss))
    rounded = stream_grad.astype(jnp.bfloat16)
    head_grad, gain_grad = lax.psum((head_local, gain_local), ("dp", "rep"))
    grad_shard = lax.psum_scatter(
        lax.dot_general(
            learn_hidden, rounded, (((0,), (0,)), ((), ())), preferred_element_type=jnp.float32
        ),
        "dp",
        scatter_dimension=0,
        tiled=True,
    )
    down_grad = lax.psum(grad_shard, "rep")
    hidden_sum = lax.dot_general(
        rounded, full_down, (((1,), (1,)), ((), ())), preferred_element_type=jnp.float32
    )
    hidden_grad = hidden_sum.astype(jnp.bfloat16)
    return (fresh_policy, targets, hidden_grad, down_grad, head_grad, gain_grad)


def solution(mesh):
    placed = (
        P(("dp", "rep"), None),
        P(("dp", "rep"), None),
        P(("dp", "rep"), None),
        P(("dp", "rep"), None),
        P("dp", None),
        P(),
        P(),
        P(("dp", "rep"), None),
        P(("dp", "rep"), None),
        P(("dp", "rep"), None),
        P(("dp", "rep"), None),
        P(("dp", "rep")),
        P(("dp", "rep")),
    )
    return jax.shard_map(
        local,
        mesh=mesh,
        in_specs=placed,
        out_specs=(
            P(("dp", "rep"), None),
            P(("dp", "rep"), None),
            P(("dp", "rep"), None),
            P("dp", None),
            P(),
            P(),
        ),
        check_vma=False,
    )
```

profile of v0, /device:TPU:8, one launch (start us, length us, event | category | flops | bytes accessed | tf_op | source)
XLA Modules:
  0.0 475.9 jit_solution(9676328896604979801)
XLA Ops:
  7.2 0.7 all-gather.2.cloned.1.call-update
  8.0 0.7 convert_element_type.21
  8.6 0.8 eq.12
  9.4 0.9 exponential_reduce_fusion
  10.3 0.7 broadcast_add_fusion
  10.9 74.4 %all-gather.2.cloned.1.call-done = bf16[4096,1024]{1,0:T(8,128)(2,1)} async-done(((bf16[256,1024]{1,0:T(8,128)(2,1)}), bf16[4096,1024]{1,0:T(8,128)(2,1)}) %all-gather.2.cloned.1.call-update) | async-done | bytes 8388624 | tf_op jit(solution)/shard_map/all_gather | solution.py:97
  85.4 9.9 %multiply_reduce_fusion.2 = (f32[640]{0:T(1024)S(1)}, f32[640,1024]{1,0:T(8,128)S(1)}) fusion(bf16[640,4096]{1,0:T(8,128)(2,1)} %param.14, bf16[4096,1024]{1,0:T(8,128)(2,1)} %all-gather.2.cloned.1.call-done, bf16[640,1024]{1,0:T(8,128)(2,1)} %param.13), kind=kOutput, calls=%fused_computation.6 | convolution fusion | flops 5371330048 | bytes 17566208 | tf_op jit(solution)/shard_map/dot_general | solution.py:98
  95.4 1.5 fusion.6
  97.3 0.1 multiply_select_fusion
  97.4 0.1 slice.177
  97.5 0.1 slice.171
  97.6 0.1 slice.167
  97.7 0.1 slice.173
  97.8 0.1 slice.169
  98.2 0.1 slice.185
  98.3 0.1 slice.181
  98.4 0.1 slice.179
  98.5 0.1 slice.182
  98.6 0.1 slice.180
  98.7 0.1 slice.192
  98.8 0.1 slice.188
  98.9 0.1 slice.186
  99.0 0.1 slice.189
  99.0 0.1 slice.187
  100.2 0.1 slice.176
  100.3 0.1 slice.165
  100.6 0.1 multiply_add_fusion.6
  101.0 0.1 pad_maximum_fusion.1
  101.4 0.1 pad.54
  101.6 0.1 pad.53
  101.7 0.1 pad.56
  102.0 0.1 pad.55
  102.3 0.1 reshape.81
  102.4 0.1 fusion.22
  102.7 1.8 multiply_reduce_fusion
  104.6 0.5 fusion
  105.1 1.2 copy-done.1
  106.3 12.7 %convolution_bitcast_fusion = f32[4096,1024]{0,1:T(8,128)} fusion(bf16[640,1024]{1,0:T(8,128)(2,1)S(1)} %fusion, bf16[640,4096]{1,0:T(8,128)(2,1)} %param.14), kind=kOutput, calls=%fused_computation | convolution fusion | flops 5368709120 | bytes 23330816 | tf_op jit(solution)/shard_map/dot_general | solution.py:126
  119.0 175.0 %reduce-scatter.2.cloned.1.call-done = f32[256,1024]{0,1:T(8,128)} async-done(((f32[4096,1024]{0,1:T(8,128)}), f32[256,1024]{0,1:T(8,128)}) %reduce-scatter.2.cloned.1.call-update) | async-done | bytes 1048592 | tf_op jit(solution)/shard_map/reduce_scatter | solution.py:125
  294.1 0.2 all-reduce.21.cloned.1.call-start
  294.3 10.9 %multiply_reduce_fusion.3 = (f32[640]{0:T(1024)S(1)}, f32[640,1024]{1,0:T(8,128)}) fusion(bf16[640,1024]{1,0:T(8,128)(2,1)} %param.15, bf16[640,4096]{1,0:T(8,128)(2,1)} %param.16, bf16[4096,1024]{1,0:T(8,128)(2,1)} %all-gather.2.cloned.1.call-done), kind=kOutput, calls=%fused_computation.11 | convolution fusion | flops 5371330048 | bytes 17566208 | tf_op jit(solution)/shard_map/dot_general | solution.py:101
  305.2 2.4 fusion.4
  307.6 11.1 %convolution_convert_fusion = bf16[640,4096]{1,0:T(8,128)(2,1)} fusion(bf16[640,1024]{1,0:T(8,128)(2,1)} %copy-done.1, bf16[4096,1024]{1,0:T(8,128)(2,1)} %all-gather.2.cloned.1.call-done), kind=kOutput, calls=%fused_computation.1 | convolution fusion | flops 5371330560 | bytes 14942208 | tf_op jit(solution)/shard_map/dot_general | solution.py:134
  318.8 2.3 fusion.1
  321.1 40.5 %psum.23 = f32[1024]{0:T(1024)} all-reduce(f32[1024]{0:T(1024)S(1)} %get-tuple-element.12), channel_id=1, replica_groups=mesh['dp'=16,'rep'=2] {'dp','rep'}, use_global_device_ids=true, to_apply=%region_12.13 | all-reduce | flops 1024 | bytes 8192 | tf_op jit(solution)/shard_map/psum | solution.py:124
  361.5 2.5 copy.19
  364.1 103.8 %all-reduce.21.cloned.1.call-done = f32[1024,19]{0,1:T(8,128)} async-done(((f32[1024,19]{0,1:T(8,128)}), f32[1024,19]{0,1:T(8,128)}) %all-reduce.21.cloned.1.call-update) | async-done | bytes 77840 | tf_op jit(solution)/shard_map/psum | solution.py:124
  467.8 1.5 copy.22
  (91 shorter events, 3.4 us)
Async XLA Ops:
  7.2 88.2 %copy-start = (bf16[1024,19]{0,1:T(8,128)(2,1)S(1)}, bf16[1024,19]{0,1:T(8,128)(2,1)}, u32[]{:S(2)}) copy-start(bf16[1024,19]{0,1:T(8,128)(2,1)} %param.18) | copy-start | bytes 116740
  7.2 78.2 %all-gather.2.cloned.1.call-start = ((), (), s32[]{:S(2)}) async-start(), calls=%async_computation.1 | async-start | bytes 8912896 | tf_op jit(solution)/shard_map/all_gather | solution.py:97
  7.9 286.2 %reduce-scatter.2.cloned.1.call-start = ((), (), s32[]{:S(2)}) async-start(), calls=%async_computation.2 | async-start | bytes 17825792 | tf_op jit(solution)/shard_map/reduce_scatter | solution.py:125
  95.3 1.8 copy-start.4
  95.3 2.0 copy-start.6
  95.3 1.9 copy-start.7
  95.3 1.9 copy-start.8
  95.3 1.9 copy-start.9
  102.3 2.3 copy-start.5
  105.1 1.2 copy-start.1
  119.0 242.5 %all-reduce.19.cloned.1.call-start = ((), (), s32[]{:S(2)}) async-start(), calls=%async_computation.3 | async-start | bytes 2097152 | tf_op jit(solution)/shard_map/psum | solution.py:133
  294.1 173.7 %all-reduce.21.cloned.1.call-start = ((), (), s32[]{:S(2)}) async-start(), calls=%async_computation.4 | async-start | bytes 196608 | tf_op jit(solution)/shard_map/psum | solution.py:124
  307.6 11.1 %copy-start.2 = (f32[640,1024]{1,0:T(8,128)S(1)}, f32[640,1024]{1,0:T(8,128)}, u32[]{:S(2)}) copy-start(f32[640,1024]{1,0:T(8,128)} %get-tuple-element.39) | copy-start | bytes 7864324
  307.6 11.1 %copy-start.3 = (bf16[640,1024]{1,0:T(8,128)(2,1)S(1)}, bf16[640,1024]{1,0:T(8,128)(2,1)}, u32[]{:S(2)}) copy-start(bf16[640,1024]{1,0:T(8,128)(2,1)} %param.15) | copy-start | bytes 3932164
Sparse Core Ops, SparseCore 0:
  10.2 75.1 all-gather.1
  119.1 174.9 reduce-scatter.1
  296.4 40.8 all-reduce.18
  343.2 124.5 all-reduce.20
where the time goes:
time: 476 us
  waiting for transfers between devices  354 us (74%)
  matrix products  52.6 us (11%)
  blocking collectives  40.5 us (9%)
  between operations  14.1 us (3%)
  local copies, waits for them, and re-layouts  10.6 us (2%)
    reduce_scatter x1, waiting for transfers between devices, local(): lax.psum_scatter(lax.dot_general(learn_hidden, rounded, (((0,), (0,)), ((...  175 us
    psum x1, waiting for transfers between devices, local(): head_grad, gain_grad = lax.psum((head_local, gain_local), ('dp', 'rep'))  104 us
    all_gather x1, waiting for transfers between devices, local(): full_down = lax.all_gather(down_weight, 'dp', axis=0, tiled=True)  74.4 us
    psum x1, blocking collectives, local(): head_grad, gain_grad = lax.psum((head_local, gain_local), ('dp', 'rep'))  40.5 us
    dot_general x1, matrix products, local(): lax.dot_general(learn_hidden, rounded, (((0,), (0,)), ((), ())), preferre...  12.7 us
    dot_general x1, matrix products, local(): lax.dot_general(rounded, full_down, (((1,), (1,)), ((), ())), preferred_e...  11.1 us
    dot_general x1, matrix products, local(): jnp.dot(fresh_hidden, full_down, preferred_element_type=jnp.float32)  10.9 us
    dot_general x1, matrix products, local(): jnp.dot(learn_hidden, full_down, preferred_element_type=jnp.float32)  9.89 us
  transfers between devices with their start and end apart: 4, of which 3 were waited for; matrix products, arithmetic and copies ran while one was open for 7% of the time, Pallas kernels for 0%

commit v1 on v0

--- a/solution.py
+++ b/solution.py
@@ -10,6 +10,19 @@
 BASELINE_COST = 0.5
 ENTROPY_COST = 0.05
 EPSILON = 1e-05
+
+
+def feed_positions_for(payload):
+    world = lax.axis_size("dp")
+    local_out = [(rr - 1, rr) for rr in range(1, world)] + [(world - 1, 0)]
+    then = payload
+    chunks = [then]
+    for _ in range(world - 1):
+        then = lax.ppermute(then, "dp", local_out)
+        chunks += [then]
+    item_now = jnp.concatenate([*reversed(chunks)], axis=0)
+    side_arr = lax.axis_index("dp")
+    return jnp.roll(item_now, (side_arr + 1) * then.shape[0], axis=0)
 
 
 def normalize(features, gain_vector):
@@ -94,7 +107,7 @@
 ):
     head_matrix = head_weight.astype(jnp.float32)
     gain_vector = norm_gain.astype(jnp.float32)
-    full_down = lax.all_gather(down_weight, "dp", axis=0, tiled=True)
+    full_down = feed_positions_for(down_weight)
     learn_stream = learn_residual.astype(jnp.float32) + jnp.dot(
         learn_hidden, full_down, preferred_element_type=jnp.float32
     )

time: 476 us -> 590 us (1.24)
  waiting for transfers between devices: 354 us -> 437 us
  local copies, waits for them, and re-layouts: 10.6 us -> 35.6 us
    ppermute x0 -> x15, waiting for transfers between devices: none -> 138 us  [feed_positions_for(): then = lax.ppermute(then, 'dp', local_out)]
    all_gather x1 -> x0, waiting for transfers between devices: 74.4 us -> none  [local(): full_down = lax.all_gather(down_weight, 'dp', axis=0, tiled=True)]
    unnamed x22 -> x91, local copies, waits for them, and re-layouts: 5.28 us -> 30.2 us
    psum x1, waiting for transfers between devices: 104 us -> 117 us  [local(): head_grad, gain_grad = lax.psum((head_local, gain_local), ('dp', 'rep'))]
    reduce_scatter x1, waiting for transfers between devices: 175 us -> 183 us  [local(): lax.psum_scatter(lax.dot_general(learn_hidden, rounded, (((0,), (0,)), ((...]
  transfers between devices with their start and end apart: 4 -> 18, of which waited for: 3 -> 17; matrix products, arithmetic and copies ran while one was open for 7% -> 7% of each run, Pallas kernels for 0% -> 0%
where the time goes in v1:
time: 590 us; the launch traced here: 589 us
  waiting for transfers between devices  437 us (74%)
  matrix products  57.7 us (10%)
  blocking collectives  40.1 us (7%)
  local copies, waits for them, and re-layouts  35.6 us (6%)
  between operations  14.5 us (2%)
    reduce_scatter x1, waiting for transfers between devices, local(): lax.psum_scatter(lax.dot_general(learn_hidden, rounded, (((0,), (0,)), ((...  183 us
    ppermute x15, waiting for transfers between devices, feed_positions_for(): then = lax.ppermute(then, 'dp', local_out)  138 us
    psum x1, waiting for transfers between devices, local(): head_grad, gain_grad = lax.psum((head_local, gain_local), ('dp', 'rep'))  117 us
    psum x1, blocking collectives, local(): head_grad, gain_grad = lax.psum((head_local, gain_local), ('dp', 'rep'))  40.1 us
    unnamed x91, local copies, waits for them, and re-layouts  30.2 us
    dot_general x1, matrix products, local(): jnp.dot(learn_hidden, full_down, preferred_element_type=jnp.float32)  13.4 us
    dot_general x1, matrix products, local(): lax.dot_general(learn_hidden, rounded, (((0,), (0,)), ((), ())), preferre...  12 us
    dot_general x1, matrix products, local(): jnp.dot(fresh_hidden, full_down, preferred_element_type=jnp.float32)  12 us
  transfers between devices with their start and end apart: 18, of which 17 were waited for; matrix products, arithmetic and copies ran while one was open for 7% of the time, Pallas kernels for 0%

profile of v1, /device:TPU:8, one launch (start us, length us, event | category | flops | bytes accessed | tf_op | source)
XLA Modules:
  0.0 589.4 jit_solution(14806851062818794630)
XLA Ops:
  7.3 9.7 %collective-permute-done = bf16[256,1024]{1,0:T(8,128)(2,1)S(1)} collective-permute-done((bf16[256,1024]{1,0:T(8,128)(2,1)}, bf16[256,1024]{1,0:T(8,128)(2,1)S(1)}, u32[]{:S(2)}, u32[]{:S(2)}) %collective-permute-start) | collective-permute-done | bytes 524320 | tf_op jit(solution)/shard_map/ppermute | solution.py:21
  17.0 9.5 %collective-permute-done.1 = bf16[256,1024]{1,0:T(8,128)(2,1)S(1)} collective-permute-done((bf16[256,1024]{1,0:T(8,128)(2,1)S(1)}, bf16[256,1024]{1,0:T(8,128)(2,1)S(1)}, u32[]{:S(2)}, u32[]{:S(2)}) %collective-permute-start.1) | collective-permute-done | bytes 524320 | tf_op jit(solution)/shard_map/ppermute | solution.py:21
  26.5 9.5 %collective-permute-done.2 = bf16[256,1024]{1,0:T(8,128)(2,1)S(1)} collective-permute-done((bf16[256,1024]{1,0:T(8,128)(2,1)S(1)}, bf16[256,1024]{1,0:T(8,128)(2,1)S(1)}, u32[]{:S(2)}, u32[]{:S(2)}) %collective-permute-start.2) | collective-permute-done | bytes 524320 | tf_op jit(solution)/shard_map/ppermute | solution.py:21
  36.0 9.5 %collective-permute-done.3 = bf16[256,1024]{1,0:T(8,128)(2,1)S(1)} collective-permute-done((bf16[256,1024]{1,0:T(8,128)(2,1)S(1)}, bf16[256,1024]{1,0:T(8,128)(2,1)S(1)}, u32[]{:S(2)}, u32[]{:S(2)}) %collective-permute-start.3) | collective-permute-done | bytes 524320 | tf_op jit(solution)/shard_map/ppermute | solution.py:21
  45.5 9.5 %collective-permute-done.4 = bf16[256,1024]{1,0:T(8,128)(2,1)S(1)} collective-permute-done((bf16[256,1024]{1,0:T(8,128)(2,1)S(1)}, bf16[256,1024]{1,0:T(8,128)(2,1)S(1)}, u32[]{:S(2)}, u32[]{:S(2)}) %collective-permute-start.4) | collective-permute-done | bytes 524320 | tf_op jit(solution)/shard_map/ppermute | solution.py:21
  55.0 9.5 %collective-permute-done.5 = bf16[256,1024]{1,0:T(8,128)(2,1)S(1)} collective-permute-done((bf16[256,1024]{1,0:T(8,128)(2,1)S(1)}, bf16[256,1024]{1,0:T(8,128)(2,1)S(1)}, u32[]{:S(2)}, u32[]{:S(2)}) %collective-permute-start.5) | collective-permute-done | bytes 524320 | tf_op jit(solution)/shard_map/ppermute | solution.py:21
  64.5 0.8 copy-done.3
  65.3 9.5 %collective-permute-done.6 = bf16[256,1024]{1,0:T(8,128)(2,1)S(1)} collective-permute-done((bf16[256,1024]{1,0:T(8,128)(2,1)S(1)}, bf16[256,1024]{1,0:T(8,128)(2,1)S(1)}, u32[]{:S(2)}, u32[]{:S(2)}) %collective-permute-start.6) | collective-permute-done | bytes 524320 | tf_op jit(solution)/shard_map/ppermute | solution.py:21
  74.9 0.8 copy-done.5
  75.7 9.5 %collective-permute-done.7 = bf16[256,1024]{1,0:T(8,128)(2,1)S(1)} collective-permute-done((bf16[256,1024]{1,0:T(8,128)(2,1)S(1)}, bf16[256,1024]{1,0:T(8,128)(2,1)S(1)}, u32[]{:S(2)}, u32[]{:S(2)}) %collective-permute-start.7) | collective-permute-done | bytes 524320 | tf_op jit(solution)/shard_map/ppermute | solution.py:21
  86.0 9.5 %collective-permute-done.8 = bf16[256,1024]{1,0:T(8,128)(2,1)S(1)} collective-permute-done((bf16[256,1024]{1,0:T(8,128)(2,1)S(1)}, bf16[256,1024]{1,0:T(8,128)(2,1)S(1)}, u32[]{:S(2)}, u32[]{:S(2)}) %collective-permute-start.8) | collective-permute-done | bytes 524320 | tf_op jit(solution)/shard_map/ppermute | solution.py:21
  95.5 0.8 copy-done.9
  96.3 9.5 %collective-permute-done.9 = bf16[256,1024]{1,0:T(8,128)(2,1)S(1)} collective-permute-done((bf16[256,1024]{1,0:T(8,128)(2,1)S(1)}, bf16[256,1024]{1,0:T(8,128)(2,1)S(1)}, u32[]{:S(2)}, u32[]{:S(2)}) %collective-permute-start.9) | collective-permute-done | bytes 524320 | tf_op jit(solution)/shard_map/ppermute | solution.py:21
  106.6 9.5 %collective-permute-done.10 = bf16[256,1024]{1,0:T(8,128)(2,1)S(1)} collective-permute-done((bf16[256,1024]{1,0:T(8,128)(2,1)S(1)}, bf16[256,1024]{1,0:T(8,128)(2,1)S(1)}, u32[]{:S(2)}, u32[]{:S(2)}) %collective-permute-start.10) | collective-permute-done | bytes 524320 | tf_op jit(solution)/shard_map/ppermute | solution.py:21
  116.9 9.5 %collective-permute-done.11 = bf16[256,1024]{1,0:T(8,128)(2,1)S(1)} collective-permute-done((bf16[256,1024]{1,0:T(8,128)(2,1)S(1)}, bf16[256,1024]{1,0:T(8,128)(2,1)S(1)}, u32[]{:S(2)}, u32[]{:S(2)}) %collective-permute-start.11) | collective-permute-done | bytes 524320 | tf_op jit(solution)/shard_map/ppermute | solution.py:21
  127.2 9.5 %collective-permute-done.12 = bf16[256,1024]{1,0:T(8,128)(2,1)S(1)} collective-permute-done((bf16[256,1024]{1,0:T(8,128)(2,1)S(1)}, bf16[256,1024]{1,0:T(8,128)(2,1)S(1)}, u32[]{:S(2)}, u32[]{:S(2)}) %collective-permute-start.12) | collective-permute-done | bytes 524320 | tf_op jit(solution)/shard_map/ppermute | solution.py:21
  137.5 9.6 %collective-permute-done.13 = bf16[256,1024]{1,0:T(8,128)(2,1)} collective-permute-done((bf16[256,1024]{1,0:T(8,128)(2,1)S(1)}, bf16[256,1024]{1,0:T(8,128)(2,1)}, u32[]{:S(2)}, u32[]{:S(2)}) %collective-permute-start.13) | collective-permute-done | bytes 524320 | tf_op jit(solution)/shard_map/ppermute | solution.py:21
  147.1 2.4 copy.20
  151.0 0.9 exponential_reduce_fusion
  151.9 0.8 broadcast_add_fusion
  152.7 4.2 collective-permute-done.14
  156.9 1.1 constant_dynamic-update-slice_fusion.31
  158.0 1.1 constant_dynamic-update-slice_fusion.30
  159.1 1.1 constant_dynamic-update-slice_fusion.29
  160.2 1.1 constant_dynamic-update-slice_fusion.28
  161.2 1.1 constant_dynamic-update-slice_fusion.27
  162.3 1.1 constant_dynamic-update-slice_fusion.26
  163.4 1.1 constant_dynamic-update-slice_fusion.25
  164.5 1.1 constant_dynamic-update-slice_fusion.24
  165.6 1.1 constant_dynamic-update-slice_fusion.23
  166.6 1.1 constant_dynamic-update-slice_fusion.22
  168.0 1.1 constant_dynamic-update-slice_fusion.15
  169.1 1.1 constant_dynamic-update-slice_fusion.14
  170.9 13.4 %multiply_reduce_fusion.2 = (f32[640]{0:T(1024)S(1)}, f32[640,1024]{0,1:T(8,128)S(1)}) fusion(bf16[640,4096]{1,0:T(8,128)(2,1)} %param.14, bf16[8192,1024]{1,0:T(8,128)(2,1)S(1)} %constant_dynamic-update-slice_fusion, s32[]{:T(128)S(6)} %select_n.34, bf16[640,1024]{0,1:T(8,128)(2,1)S(1)} %copy-done.19), kind=kOutput, calls=%fused_computation.14 | convolution fusion | flops 5371330048 | bytes 17566212 | tf_op jit(solution)/shard_map/dot_general | solution.py:111
  184.4 1.2 fusion.15
  191.4 1.9 multiply_reduce_fusion
  193.9 1.1 copy-done.20
  195.1 12.0 %convolution_bitcast_fusion = f32[4096,1024]{0,1:T(8,128)} fusion(bf16[640,1024]{0,1:T(8,128)(2,1)S(1)} %fusion.9, bf16[640,4096]{1,0:T(8,128)(2,1)} %param.14), kind=kOutput, calls=%fused_computation | convolution fusion | flops 5368709120 | bytes 23330816 | tf_op jit(solution)/shard_map/dot_general | solution.py:139
  207.2 2.5 copy.19
  209.7 12.0 %multiply_reduce_fusion.3 = (f32[640]{0:T(1024)S(1)}, f32[1024,640]{1,0:T(8,128)}) fusion(bf16[640,1024]{0,1:T(8,128)(2,1)} %copy.19, bf16[640,4096]{1,0:T(8,128)(2,1)} %param.16, bf16[8192,1024]{1,0:T(8,128)(2,1)} %copy-done.22, s32[]{:T(128)S(6)} %select_n.34), kind=kOutput, calls=%fused_computation.18 | convolution fusion | flops 5371330048 | bytes 17566212 | tf_op jit(solution)/shard_map/dot_general | solution.py:114
  221.6 3.2 fusion.13
  224.8 182.7 %reduce-scatter.2.cloned.1.call-done = f32[256,1024]{0,1:T(8,128)} async-done(((f32[4096,1024]{0,1:T(8,128)}), f32[256,1024]{0,1:T(8,128)}) %reduce-scatter.2.cloned.1.call-update) | async-done | bytes 1048592 | tf_op jit(solution)/shard_map/reduce_scatter | solution.py:138
  407.6 10.3 %fusion.6 = bf16[640,4096]{1,0:T(8,128)(2,1)} fusion(bf16[640,1024]{0,1:T(8,128)(2,1)} %copy-done.20, bf16[8192,1024]{1,0:T(8,128)(2,1)} %copy-done.22, s32[]{:T(128)S(6)} %select_n.34), kind=kOutput, calls=%fused_computation.7 | convolution fusion | flops 5371330560 | bytes 14942212 | tf_op jit(solution)/shard_map/dot_general | solution.py:147
  417.9 3.7 fusion.10
  421.6 40.1 %psum.23 = f32[1024]{0:T(1024)} all-reduce(f32[1024]{0:T(1024)S(1)} %get-tuple-element.12), channel_id=1, replica_groups=mesh['dp'=16,'rep'=2] {'dp','rep'}, use_global_device_ids=true, to_apply=%region_12.13 | all-reduce | flops 1024 | bytes 8192 | tf_op jit(solution)/shard_map/psum | solution.py:137
  461.7 2.5 copy.23
  464.3 117.1 %all-reduce.21.cloned.1.call-done = f32[1024,19]{0,1:T(8,128)} async-done(((f32[1024,19]{0,1:T(8,128)}), f32[1024,19]{0,1:T(8,128)}) %all-reduce.21.cloned.1.call-update) | async-done | bytes 77840 | tf_op jit(solution)/shard_map/psum | solution.py:137
  581.4 1.5 copy.58
  (188 shorter events, 12.7 us)
Async XLA Ops:
  7.2 177.2 %copy-start = (bf16[1024,19]{0,1:T(8,128)(2,1)S(1)}, bf16[1024,19]{0,1:T(8,128)(2,1)}, u32[]{:S(2)}) copy-start(bf16[1024,19]{0,1:T(8,128)(2,1)} %param.18) | copy-start | bytes 116740
  7.2 160.8 %copy-start.2 = (bf16[256,1024]{1,0:T(8,128)(2,1)S(1)}, bf16[256,1024]{1,0:T(8,128)(2,1)}, u32[]{:S(2)}) copy-start(bf16[256,1024]{1,0:T(8,128)(2,1)} %param.17) | copy-start | bytes 1572868
  7.2 400.3 %reduce-scatter.2.cloned.1.call-start = ((), (), s32[]{:S(2)}) async-start(), calls=%async_computation.1 | async-start | bytes 17825792 | tf_op jit(solution)/shard_map/reduce_scatter | solution.py:138
  7.2 9.8 %collective-permute-start = (bf16[256,1024]{1,0:T(8,128)(2,1)}, bf16[256,1024]{1,0:T(8,128)(2,1)S(1)}, u32[]{:S(2)}, u32[]{:S(2)}) collective-permute-start(bf16[256,1024]{1,0:T(8,128)(2,1)} %param.17), channel_id=1, source_target_pairs={{0,2},{2,4},{4,6},{6,8},{8,10},{10,12},{12,14},{14,16},{16,18},{18... | collective-permute-start | bytes 1572872 | tf_op jit(solution)/shard_map/ppermute | solution.py:21
  17.0 9.5 %collective-permute-start.1 = (bf16[256,1024]{1,0:T(8,128)(2,1)S(1)}, bf16[256,1024]{1,0:T(8,128)(2,1)S(1)}, u32[]{:S(2)}, u32[]{:S(2)}) collective-permute-start(bf16[256,1024]{1,0:T(8,128)(2,1)S(1)} %collective-permute-done), channel_id=1, source_target_pairs={{0,2},{2,4},{4,6},{6,8},{8,10},{10,12},{12,14},{14,16},{16,18},{18... | collective-permute-start | bytes 1572872 | tf_op jit(solution)/shard_map/ppermute | solution.py:21
  26.5 9.5 %collective-permute-start.2 = (bf16[256,1024]{1,0:T(8,128)(2,1)S(1)}, bf16[256,1024]{1,0:T(8,128)(2,1)S(1)}, u32[]{:S(2)}, u32[]{:S(2)}) collective-permute-start(bf16[256,1024]{1,0:T(8,128)(2,1)S(1)} %collective-permute-done.1), channel_id=1, source_target_pairs={{0,2},{2,4},{4,6},{6,8},{8,10},{10,12},{12,14},{14,16},{16,18},{18... | collective-permute-start | bytes 1572872 | tf_op jit(solution)/shard_map/ppermute | solution.py:21
  36.0 9.5 %collective-permute-start.3 = (bf16[256,1024]{1,0:T(8,128)(2,1)S(1)}, bf16[256,1024]{1,0:T(8,128)(2,1)S(1)}, u32[]{:S(2)}, u32[]{:S(2)}) collective-permute-start(bf16[256,1024]{1,0:T(8,128)(2,1)S(1)} %collective-permute-done.2), channel_id=1, source_target_pairs={{0,2},{2,4},{4,6},{6,8},{8,10},{10,12},{12,14},{14,16},{16,18},{18... | collective-permute-start | bytes 1572872 | tf_op jit(solution)/shard_map/ppermute | solution.py:21
  45.5 9.5 %collective-permute-start.4 = (bf16[256,1024]{1,0:T(8,128)(2,1)S(1)}, bf16[256,1024]{1,0:T(8,128)(2,1)S(1)}, u32[]{:S(2)}, u32[]{:S(2)}) collective-permute-start(bf16[256,1024]{1,0:T(8,128)(2,1)S(1)} %collective-permute-done.3), channel_id=1, source_target_pairs={{0,2},{2,4},{4,6},{6,8},{8,10},{10,12},{12,14},{14,16},{16,18},{18... | collective-permute-start | bytes 1572872 | tf_op jit(solution)/shard_map/ppermute | solution.py:21
  55.0 9.5 %collective-permute-start.5 = (bf16[256,1024]{1,0:T(8,128)(2,1)S(1)}, bf16[256,1024]{1,0:T(8,128)(2,1)S(1)}, u32[]{:S(2)}, u32[]{:S(2)}) collective-permute-start(bf16[256,1024]{1,0:T(8,128)(2,1)S(1)} %collective-permute-done.4), channel_id=1, source_target_pairs={{0,2},{2,4},{4,6},{6,8},{8,10},{10,12},{12,14},{14,16},{16,18},{18... | collective-permute-start | bytes 1572872 | tf_op jit(solution)/shard_map/ppermute | solution.py:21
  64.5 0.8 copy-start.3
  65.3 9.5 %collective-permute-start.6 = (bf16[256,1024]{1,0:T(8,128)(2,1)S(1)}, bf16[256,1024]{1,0:T(8,128)(2,1)S(1)}, u32[]{:S(2)}, u32[]{:S(2)}) collective-permute-start(bf16[256,1024]{1,0:T(8,128)(2,1)S(1)} %collective-permute-done.5), channel_id=1, source_target_pairs={{0,2},{2,4},{4,6},{6,8},{8,10},{10,12},{12,14},{14,16},{16,18},{18... | collective-permute-start | bytes 1572872 | tf_op jit(solution)/shard_map/ppermute | solution.py:21
  74.8 0.8 copy-start.5
  75.7 9.5 %collective-permute-start.7 = (bf16[256,1024]{1,0:T(8,128)(2,1)S(1)}, bf16[256,1024]{1,0:T(8,128)(2,1)S(1)}, u32[]{:S(2)}, u32[]{:S(2)}) collective-permute-start(bf16[256,1024]{1,0:T(8,128)(2,1)S(1)} %collective-permute-done.6), channel_id=1, source_target_pairs={{0,2},{2,4},{4,6},{6,8},{8,10},{10,12},{12,14},{14,16},{16,18},{18... | collective-permute-start | bytes 1572872 | tf_op jit(solution)/shard_map/ppermute | solution.py:21
  85.2 0.8 copy-start.7
  86.0 9.5 %collective-permute-start.8 = (bf16[256,1024]{1,0:T(8,128)(2,1)S(1)}, bf16[256,1024]{1,0:T(8,128)(2,1)S(1)}, u32[]{:S(2)}, u32[]{:S(2)}) collective-permute-start(bf16[256,1024]{1,0:T(8,128)(2,1)S(1)} %collective-permute-done.7), channel_id=1, source_target_pairs={{0,2},{2,4},{4,6},{6,8},{8,10},{10,12},{12,14},{14,16},{16,18},{18... | collective-permute-start | bytes 1572872 | tf_op jit(solution)/shard_map/ppermute | solution.py:21
  95.5 0.8 copy-start.9
  96.3 9.5 %collective-permute-start.9 = (bf16[256,1024]{1,0:T(8,128)(2,1)S(1)}, bf16[256,1024]{1,0:T(8,128)(2,1)S(1)}, u32[]{:S(2)}, u32[]{:S(2)}) collective-permute-start(bf16[256,1024]{1,0:T(8,128)(2,1)S(1)} %collective-permute-done.8), channel_id=1, source_target_pairs={{0,2},{2,4},{4,6},{6,8},{8,10},{10,12},{12,14},{14,16},{16,18},{18... | collective-permute-start | bytes 1572872 | tf_op jit(solution)/shard_map/ppermute | solution.py:21
  105.8 0.8 copy-start.11
  106.6 9.5 %collective-permute-start.10 = (bf16[256,1024]{1,0:T(8,128)(2,1)S(1)}, bf16[256,1024]{1,0:T(8,128)(2,1)S(1)}, u32[]{:S(2)}, u32[]{:S(2)}) collective-permute-start(bf16[256,1024]{1,0:T(8,128)(2,1)S(1)} %collective-permute-done.9), channel_id=1, source_target_pairs={{0,2},{2,4},{4,6},{6,8},{8,10},{10,12},{12,14},{14,16},{16,18},{18... | collective-permute-start | bytes 1572872 | tf_op jit(solution)/shard_map/ppermute | solution.py:21
  116.1 0.8 copy-start.13
  116.9 9.5 %collective-permute-start.11 = (bf16[256,1024]{1,0:T(8,128)(2,1)S(1)}, bf16[256,1024]{1,0:T(8,128)(2,1)S(1)}, u32[]{:S(2)}, u32[]{:S(2)}) collective-permute-start(bf16[256,1024]{1,0:T(8,128)(2,1)S(1)} %collective-permute-done.10), channel_id=1, source_target_pairs={{0,2},{2,4},{4,6},{6,8},{8,10},{10,12},{12,14},{14,16},{16,18},{18... | collective-permute-start | bytes 1572872 | tf_op jit(solution)/shard_map/ppermute | solution.py:21
  126.4 0.8 copy-start.15
  127.2 9.5 %collective-permute-start.12 = (bf16[256,1024]{1,0:T(8,128)(2,1)S(1)}, bf16[256,1024]{1,0:T(8,128)(2,1)S(1)}, u32[]{:S(2)}, u32[]{:S(2)}) collective-permute-start(bf16[256,1024]{1,0:T(8,128)(2,1)S(1)} %collective-permute-done.11), channel_id=1, source_target_pairs={{0,2},{2,4},{4,6},{6,8},{8,10},{10,12},{12,14},{14,16},{16,18},{18... | collective-permute-start | bytes 1572872 | tf_op jit(solution)/shard_map/ppermute | solution.py:21
  136.7 0.8 copy-start.17
  137.5 9.6 %collective-permute-start.13 = (bf16[256,1024]{1,0:T(8,128)(2,1)S(1)}, bf16[256,1024]{1,0:T(8,128)(2,1)}, u32[]{:S(2)}, u32[]{:S(2)}) collective-permute-start(bf16[256,1024]{1,0:T(8,128)(2,1)S(1)} %collective-permute-done.12), channel_id=1, source_target_pairs={{0,2},{2,4},{4,6},{6,8},{8,10},{10,12},{12,14},{14,16},{16,18},{18... | collective-permute-start | bytes 1572872 | tf_op jit(solution)/shard_map/ppermute | solution.py:21
  147.1 9.8 %collective-permute-start.14 = (bf16[256,1024]{1,0:T(8,128)(2,1)}, bf16[256,1024]{1,0:T(8,128)(2,1)}, u32[]{:S(2)}, u32[]{:S(2)}) collective-permute-start(bf16[256,1024]{1,0:T(8,128)(2,1)} %collective-permute-done.13), channel_id=1, source_target_pairs={{0,2},{2,4},{4,6},{6,8},{8,10},{10,12},{12,14},{14,16},{16,18},{18... | collective-permute-start | bytes 1572872 | tf_op jit(solution)/shard_map/ppermute | solution.py:21
  151.8 18.3 %copy-start.18 = (bf16[256,1024]{1,0:T(8,128)(2,1)S(1)}, bf16[256,1024]{1,0:T(8,128)(2,1)}, u32[]{:S(2)}) copy-start(bf16[256,1024]{1,0:T(8,128)(2,1)} %copy-done.17) | copy-start | bytes 1572868
  151.9 18.4 %copy-start.16 = (bf16[256,1024]{1,0:T(8,128)(2,1)S(1)}, bf16[256,1024]{1,0:T(8,128)(2,1)}, u32[]{:S(2)}) copy-start(bf16[256,1024]{1,0:T(8,128)(2,1)} %copy-done.15) | copy-start | bytes 1572868
  151.9 18.4 %copy-start.14 = (bf16[256,1024]{1,0:T(8,128)(2,1)S(1)}, bf16[256,1024]{1,0:T(8,128)(2,1)}, u32[]{:S(2)}) copy-start(bf16[256,1024]{1,0:T(8,128)(2,1)} %copy-done.13) | copy-start | bytes 1572868
  151.9 18.4 %copy-start.12 = (bf16[256,1024]{1,0:T(8,128)(2,1)S(1)}, bf16[256,1024]{1,0:T(8,128)(2,1)}, u32[]{:S(2)}) copy-start(bf16[256,1024]{1,0:T(8,128)(2,1)} %copy-done.11) | copy-start | bytes 1572868
  151.9 18.5 %copy-start.10 = (bf16[256,1024]{1,0:T(8,128)(2,1)S(1)}, bf16[256,1024]{1,0:T(8,128)(2,1)}, u32[]{:S(2)}) copy-start(bf16[256,1024]{1,0:T(8,128)(2,1)} %copy-done.9) | copy-start | bytes 1572868
  151.9 18.5 %copy-start.8 = (bf16[256,1024]{1,0:T(8,128)(2,1)S(1)}, bf16[256,1024]{1,0:T(8,128)(2,1)}, u32[]{:S(2)}) copy-start(bf16[256,1024]{1,0:T(8,128)(2,1)} %copy-done.7) | copy-start | bytes 1572868
  151.9 18.6 %copy-start.6 = (bf16[256,1024]{1,0:T(8,128)(2,1)S(1)}, bf16[256,1024]{1,0:T(8,128)(2,1)}, u32[]{:S(2)}) copy-start(bf16[256,1024]{1,0:T(8,128)(2,1)} %copy-done.5) | copy-start | bytes 1572868
  151.9 18.6 %copy-start.4 = (bf16[256,1024]{1,0:T(8,128)(2,1)S(1)}, bf16[256,1024]{1,0:T(8,128)(2,1)}, u32[]{:S(2)}) copy-start(bf16[256,1024]{1,0:T(8,128)(2,1)} %copy-done.3) | copy-start | bytes 1572868
  152.7 18.1 %copy-start.19 = (bf16[640,1024]{0,1:T(8,128)(2,1)S(1)}, bf16[640,1024]{0,1:T(8,128)(2,1)}, u32[]{:S(2)}) copy-start(bf16[640,1024]{0,1:T(8,128)(2,1)} %copy.20) | copy-start | bytes 3932164
  170.9 13.5 %copy-start.22 = (bf16[8192,1024]{1,0:T(8,128)(2,1)}, bf16[8192,1024]{1,0:T(8,128)(2,1)S(1)}, u32[]{:S(2)}) copy-start(bf16[8192,1024]{1,0:T(8,128)(2,1)S(1)} %constant_dynamic-update-slice_fusion) | copy-start | bytes 50331652
  170.9 14.8 %copy-start.21 = (f32[640,18]{0,1:T(8,128)S(1)}, f32[640,18]{0,1:T(8,128)}, u32[]{:S(2)}) copy-start(f32[640,18]{0,1:T(8,128)} %param.21) | copy-start | bytes 138244
  170.9 15.1 %copy-start.24 = (s32[8,80]{1,0:T(8,128)S(1)}, s32[8,80]{1,0:T(8,128)}, u32[]{:S(2)}) copy-start(s32[8,80]{1,0:T(8,128)} %param.23) | copy-start | bytes 7684
  170.9 15.1 %copy-start.25 = (f32[8,80]{1,0:T(8,128)S(1)}, f32[8,80]{1,0:T(8,128)}, u32[]{:S(2)}) copy-start(f32[8,80]{1,0:T(8,128)} %param.22) | copy-start | bytes 7684
  170.9 15.0 %copy-start.26 = (s32[8]{0:T(128)S(1)}, s32[8]{0:T(128)}, u32[]{:S(2)}) copy-start(s32[8]{0:T(128)} %param.24) | copy-start | bytes 100
  170.9 15.0 %copy-start.27 = (f32[8]{0:T(128)S(1)}, f32[8]{0:T(128)}, u32[]{:S(2)}) copy-start(f32[8]{0:T(128)} %param.25) | copy-start | bytes 100
  191.0 16.2 %copy-start.23 = (f32[8,80]{1,0:T(8,128)}, f32[8,80]{1,0:T(8,128)S(1)}, u32[]{:S(2)}) copy-start(f32[8,80]{1,0:T(8,128)S(1)} %get-tuple-element.42) | copy-start | bytes 7684
  193.9 1.1 copy-start.20
  207.1 254.6 %all-reduce.19.cloned.1.call-start = ((), (), s32[]{:S(2)}) async-start(), calls=%async_computation.2 | async-start | bytes 2097152 | tf_op jit(solution)/shard_map/psum | solution.py:146
  407.6 10.4 %copy-start.1 = (bf16[640,1024]{0,1:T(8,128)(2,1)S(1)}, bf16[640,1024]{0,1:T(8,128)(2,1)}, u32[]{:S(2)}) copy-start(bf16[640,1024]{0,1:T(8,128)(2,1)} %copy.19) | copy-start | bytes 3932164
  407.6 173.8 %all-reduce.21.cloned.1.call-start = ((), (), s32[]{:S(2)}) async-start(), calls=%async_computation.3 | async-start | bytes 196608 | tf_op jit(solution)/shard_map/psum | solution.py:137
Sparse Core Ops, SparseCore 0:
  207.3 200.2 reduce-scatter.1
  409.8 40.8 all-reduce.18
  456.9 124.4 all-reduce.20
